TPU v7x, 512 devices: a whole 4x4x16 slice. The times are simulated.
512 devices in a mesh: row: 16 (over x, y), col: 32 (over z, core).
Axes of the slice: x: 4, y: 4, z: 16, core: 2. Of those that a mesh axis runs over, the one named last changes fastest.
Arguments:
- front: bfloat16 [16384, 16384], P('row', 'col'), may hold values from -0.046875 to 0.046875
- diag_inverse: float32 [128, 128, 128], P('row'), may hold values from -0.25 to 1.5
- load: float32 [8, 16384], P(None, 'row'), may hold values from -6 to 6
- panel_order: int32 [128], replicated, may hold values from 0 to 127, each once
- tie: float32 [32, 16384], P('col', 'row'), may hold values from 0.5 to 1.5
- mass: float32 [32, 16384], P('col', 'row'), may hold values from 0.5 to 6
- modes: bfloat16 [1024, 32, 16384], P(None, 'col', 'row'), may hold values from -0.0234375 to 0.0234375
Outputs:
- front_solution: float32 [8, 16384], P(None, 'row')
- residual_vectors: float32 [8, 32, 16384], P(None, 'col', 'row')
All inputs are finite; a program needn't handle non-finite values.
Results may differ from a plain program's by a relative error of at most 0.0049.
Values may be sent and summed in bfloat16 or wider, within the bound.
No kernel may reach another device: no remote copies, remote signals or barrier semaphores. Data moves between devices by JAX's collectives and lax.ppermute only.
A program may use at most 64 MiB of HBM per device.

v0:
```python
import jax
import jax.numpy as jnp
from jax import lax
from jax.sharding import PartitionSpec as P

LEVELS = 4
highest = lax.Precision.HIGHEST


def on_device(front, diag_inverse, load, panel_order, tie, mass, modes):
    vectors = load.shape[0]
    block_size = diag_inverse.shape[1]
    local_panels = diag_inverse.shape[0]
    rows_local = front.shape[0]
    cols_local = front.shape[1]
    panels = panel_order.shape[0]
    row_at = lax.axis_index("row")
    col_at = lax.axis_index("col")
    counting = jnp.arange(panels, dtype=jnp.int32)
    matches = panel_order[:, None] == counting[None, :]
    ranks = jnp.sum(jnp.where(matches, counting[:, None], 0), axis=0)
    levels_of = ranks // (panels // LEVELS)
    position_level = jnp.repeat(levels_of, block_size)
    row_level = lax.dynamic_slice_in_dim(position_level, row_at * rows_local, rows_local, 0)
    pending = jnp.zeros((vectors, rows_local), jnp.float32)
    forward_out = jnp.zeros((vectors, rows_local), jnp.float32)
    for level in range(LEVELS):
        if level > 0:
            total_sum = lax.psum(pending, "col")
        else:
            total_sum = pending
        remain = (load - total_sum).reshape(vectors, local_panels, block_size)
        candidate = jnp.einsum("vpj,pij->vpi", remain, diag_inverse, precision=highest).reshape(
            vectors, rows_local
        )
        chosen = row_level[None, :] == level
        forward_out = jnp.where(chosen, candidate, forward_out)
        if level < LEVELS - 1:
            fresh = jnp.where(chosen, forward_out, 0.0).astype(jnp.bfloat16)
            whole = lax.all_gather(fresh, "row", axis=1, tiled=True)
            mine = lax.dynamic_slice_in_dim(whole, col_at * cols_local, cols_local, 1)
            pending = pending + jnp.dot(mine, front.T, preferred_element_type=jnp.float32)
    back_pending = jnp.zeros((vectors, cols_local), jnp.float32)
    back_out = jnp.zeros((vectors, rows_local), jnp.float32)
    for level in reversed(range(LEVELS)):
        if level < LEVELS - 1:
            column_sum = lax.psum(back_pending, "row")
            full_sum = lax.all_gather(column_sum, "col", axis=1, tiled=True)
            here = lax.dynamic_slice_in_dim(full_sum, row_at * rows_local, rows_local, 1)
        else:
            here = jnp.zeros((vectors, rows_local), jnp.float32)
        remain = (forward_out - here).reshape(vectors, local_panels, block_size)
        candidate = jnp.einsum("vpj,pji->vpi", remain, diag_inverse, precision=highest).reshape(
            vectors, rows_local
        )
        chosen = row_level[None, :] == level
        back_out = jnp.where(chosen, candidate, back_out)
        if level > 0:
            fresh = jnp.where(chosen, back_out, 0.0).astype(jnp.bfloat16)
            back_pending = back_pending + jnp.dot(fresh, front, preferred_element_type=jnp.float32)
    static = tie[None, :, :] * back_out[:, None, :]
    weighted = (mass[None, :, :] * static).astype(jnp.bfloat16).reshape(vectors, -1)
    mode_rows = modes.reshape(modes.shape[0], -1)
    partial_coords = lax.dot_general(
        weighted, mode_rows, (((1,), (1,)), ((), ())), preferred_element_type=jnp.float32
    )
    coords = lax.psum(partial_coords, ("row", "col"))
    correction = jnp.dot(coords.astype(jnp.bfloat16), mode_rows, preferred_element_type=jnp.float32)
    return (back_out, static - correction.reshape(static.shape))


def solution(mesh):
    in_specs = (
        P("row", "col"),
        P("row", None, None),
        P(None, "row"),
        P(),
        P("col", "row"),
        P("col", "row"),
        P(None, "col", "row"),
    )
    out_specs = (P(None, "row"), P(None, "col", "row"))
    return jax.shard_map(
        on_device, mesh=mesh, in_specs=in_specs, out_specs=out_specs, check_vma=False
    )
```

profile of v0, /device:TPU:1, one launch (start us, length us, event | category | flops | bytes accessed | tf_op | source)
XLA Modules:
  0.0 765.4 jit_solution(5559178636949547583)
XLA Ops:
  0.6 0.0 copy-start
  0.6 0.0 copy-start.1
  0.7 0.0 copy-start.2
  0.7 0.9 select_reduce_fusion
  1.6 0.1 broadcast_bitcast_fusion
  1.7 2.0 select_convert_fusion.5
  3.7 19.7 %all_gather.18 = bf16[8,16384]{1,0:T(8,128)(2,1)S(1)} all-gather(bf16[8,1024]{1,0:T(8,128)(2,1)S(1)} %get-tuple-element.14), channel_id=1, replica_groups=mesh['row'=16,'col'=32] {'row'}, dimensions={1}, use_global_device_ids=true | all-gather | bytes 278528 | tf_op jit(solution)/shard_map/all_gather | solution.py:40
  23.3 1.6 fusion.64
  24.9 99.0 %psum.49 = f32[8,1024]{1,0:T(8,128)S(1)} all-reduce(f32[8,1024]{1,0:T(8,128)S(1)} %fusion.64), channel_id=1, replica_groups=mesh['row'=16,'col'=32] {'col'}, use_global_device_ids=true, to_apply=%region_1.2 | all-reduce | flops 8192 | bytes 65536 | tf_op jit(solution)/shard_map/psum | solution.py:29
  123.9 0.0 copy-done.2
  123.9 2.0 select_convert_fusion.4
  125.9 17.9 %all_gather.19 = bf16[8,16384]{1,0:T(8,128)(2,1)S(1)} all-gather(bf16[8,1024]{1,0:T(8,128)(2,1)S(1)} %get-tuple-element.8), channel_id=1, replica_groups=mesh['row'=16,'col'=32] {'row'}, dimensions={1}, use_global_device_ids=true | all-gather | bytes 278528 | tf_op jit(solution)/shard_map/all_gather | solution.py:40
  143.8 0.0 copy-done.1
  143.8 0.4 convolution_add_fusion.1
  144.2 95.2 %psum.50 = f32[8,1024]{1,0:T(8,128)S(1)} all-reduce(f32[8,1024]{1,0:T(8,128)S(1)} %convolution_add_fusion.1), channel_id=1, replica_groups=mesh['row'=16,'col'=32] {'col'}, use_global_device_ids=true, to_apply=%region_2.3 | all-reduce | flops 8192 | bytes 65536 | tf_op jit(solution)/shard_map/psum | solution.py:29
  239.4 2.0 select_convert_fusion.3
  241.4 16.6 %all_gather.20 = bf16[8,16384]{1,0:T(8,128)(2,1)S(1)} all-gather(bf16[8,1024]{1,0:T(8,128)(2,1)S(1)} %get-tuple-element.17), channel_id=1, replica_groups=mesh['row'=16,'col'=32] {'row'}, dimensions={1}, use_global_device_ids=true | all-gather | bytes 278528 | tf_op jit(solution)/shard_map/all_gather | solution.py:40
  258.0 0.4 convolution_add_fusion
  258.4 94.9 %psum.51 = f32[8,1024]{1,0:T(8,128)S(1)} all-reduce(f32[8,1024]{1,0:T(8,128)S(1)} %convolution_add_fusion), channel_id=1, replica_groups=mesh['row'=16,'col'=32] {'col'}, use_global_device_ids=true, to_apply=%region_3.4 | all-reduce | flops 8192 | bytes 65536 | tf_op jit(solution)/shard_map/psum | solution.py:29
  353.3 2.0 bitcast_select_fusion.5
  355.3 1.6 fusion.22
  356.9 0.2 fusion.40
  357.1 58.2 %psum.52 = f32[8,512]{1,0:T(8,128)S(1)} all-reduce(f32[8,512]{1,0:T(8,128)S(1)} %fusion.40), channel_id=1, replica_groups=mesh['row'=16,'col'=32] {'row'}, use_global_device_ids=true, to_apply=%region_4.5 | all-reduce | flops 4096 | bytes 32768 | tf_op jit(solution)/shard_map/psum | solution.py:47
  415.3 45.4 %all_gather.21 = f32[8,16384]{1,0:T(8,128)S(1)} all-gather(f32[8,512]{1,0:T(8,128)S(1)} %psum.52), channel_id=1, replica_groups=mesh['row'=16,'col'=32] {'col'}, dimensions={1}, use_global_device_ids=true | all-gather | bytes 540672 | tf_op jit(solution)/shard_map/all_gather | solution.py:48
  460.8 1.6 bitcast_select_fusion.3
  462.3 0.2 convolution_add_fusion.3
  462.6 0.0 copy-start.4
  462.6 0.0 copy-start.5
  462.6 55.9 %psum.53 = f32[8,512]{1,0:T(8,128)S(1)} all-reduce(f32[8,512]{1,0:T(8,128)S(1)} %convolution_add_fusion.3), channel_id=1, replica_groups=mesh['row'=16,'col'=32] {'row'}, use_global_device_ids=true, to_apply=%region_5.6 | all-reduce | flops 4096 | bytes 32768 | tf_op jit(solution)/shard_map/psum | solution.py:47
  518.5 44.6 %all_gather.22 = f32[8,16384]{1,0:T(8,128)S(1)} all-gather(f32[8,512]{1,0:T(8,128)S(1)} %psum.53), channel_id=1, replica_groups=mesh['row'=16,'col'=32] {'col'}, dimensions={1}, use_global_device_ids=true | all-gather | bytes 540672 | tf_op jit(solution)/shard_map/all_gather | solution.py:48
  563.1 1.6 fusion.18
  564.6 0.2 convolution_add_fusion.2
  564.9 55.8 %psum.54 = f32[8,512]{1,0:T(8,128)S(1)} all-reduce(f32[8,512]{1,0:T(8,128)S(1)} %convolution_add_fusion.2), channel_id=1, replica_groups=mesh['row'=16,'col'=32] {'row'}, use_global_device_ids=true, to_apply=%region_6.7 | all-reduce | flops 4096 | bytes 32768 | tf_op jit(solution)/shard_map/psum | solution.py:47
  620.6 42.0 %all_gather.23 = f32[8,16384]{1,0:T(8,128)S(1)} all-gather(f32[8,512]{1,0:T(8,128)S(1)} %psum.54), channel_id=1, replica_groups=mesh['row'=16,'col'=32] {'col'}, dimensions={1}, use_global_device_ids=true | all-gather | bytes 540672 | tf_op jit(solution)/shard_map/all_gather | solution.py:48
  662.6 1.6 bitcast_select_fusion.1
  664.2 0.0 copy-start.3
  664.2 0.0 copy-done
  664.2 0.0 copy-done.4
  664.2 0.0 copy-done.5
  664.2 0.6 fusion.2
  664.8 99.5 %psum.55 = bf16[8,1024]{1,0:T(8,128)(2,1)S(1)} all-reduce(f32[8,1024]{1,0:T(8,128)S(1)} %fusion.2), channel_id=1, replica_groups=mesh['row'=16,'col'=32] {'row','col'}, use_global_device_ids=true, to_apply=%region_7.8 | all-reduce | flops 8192 | bytes 49152 | tf_op jit(solution)/shard_map/psum | solution.py:67
  764.4 0.4 fusion.7
  764.8 0.0 copy-done.3
  764.8 0.7 copy.11
  (2 shorter events, 0.0 us)
Async XLA Ops:
  0.6 663.6 %copy-start = (bf16[1024,1,1024]{2,0,1:T(8,128)(2,1)S(1)}, bf16[1024,1,1024]{2,0,1:T(8,128)(2,1)}, u32[]{:S(2)}) copy-start(bf16[1024,1,1024]{2,0,1:T(8,128)(2,1)} %param.13) | copy-start | bytes 6291460
  0.6 143.2 %copy-start.1 = (bf16[1024,512]{1,0:T(8,128)(2,1)S(1)}, bf16[1024,512]{1,0:T(8,128)(2,1)}, u32[]{:S(2)}) copy-start(bf16[1024,512]{1,0:T(8,128)(2,1)} %param.7) | copy-start | bytes 3145732
  0.7 123.3 %copy-start.2 = (f32[8,1024]{1,0:T(8,128)S(1)}, f32[8,1024]{1,0:T(8,128)}, u32[]{:S(2)}) copy-start(f32[8,1024]{1,0:T(8,128)} %param.9) | copy-start | bytes 98308
  462.6 201.6 %copy-start.4 = (f32[1,1024]{1,0:T(1,128)S(1)}, f32[1,1024]{1,0:T(1,128)}, u32[]{:S(2)}) copy-start(f32[1,1024]{1,0:T(1,128)} %param.11) | copy-start | bytes 12292
  462.6 201.6 %copy-start.5 = (f32[1,1024]{1,0:T(1,128)S(1)}, f32[1,1024]{1,0:T(1,128)}, u32[]{:S(2)}) copy-start(f32[1,1024]{1,0:T(1,128)} %param.12) | copy-start | bytes 12292
  664.2 100.6 %copy-start.3 = (f32[8,1024]{1,0:T(8,128)}, f32[8,1024]{1,0:T(8,128)S(1)}, u32[]{:S(2)}) copy-start(f32[8,1024]{1,0:T(8,128)S(1)} %get-tuple-element.23) | copy-start | bytes 98308
where the time goes:
time: 766 us; the launch traced here: 765 us
  blocking collectives  745 us (97%)
  matrix products  18.2 us (2%)
    psum x3, blocking collectives, on_device(): total_sum = lax.psum(pending, 'col')  289 us
    psum x3, blocking collectives, on_device(): column_sum = lax.psum(back_pending, 'row')  170 us
    all_gather x3, blocking collectives, on_device(): full_sum = lax.all_gather(column_sum, 'col', axis=1, tiled=True)  132 us
    psum x1, blocking collectives, on_device(): coords = lax.psum(partial_coords, ('row', 'col'))  99.5 us
    all_gather x3, blocking collectives, on_device(): whole = lax.all_gather(fresh, 'row', axis=1, tiled=True)  54.2 us

commit v1 on v0

--- a/solution.py
+++ b/solution.py
@@ -45,7 +45,9 @@
     for level in reversed(range(LEVELS)):
         if level < LEVELS - 1:
             column_sum = lax.psum(back_pending, "row")
-            full_sum = lax.all_gather(column_sum, "col", axis=1, tiled=True)
+            full_sum = jnp.concatenate(
+                lax.all_to_all(jnp.stack([column_sum] * lax.axis_size("col")), "col", 0, 0), axis=1
+            )
             here = lax.dynamic_slice_in_dim(full_sum, row_at * rows_local, rows_local, 1)
         else:
             here = jnp.zeros((vectors, rows_local), jnp.float32)

time: 766 us -> 794 us (1.037)
  blocking collectives: 745 us -> 772 us
    all_to_all x0 -> x3, blocking collectives: none -> 160 us  [on_device(): lax.all_to_all(jnp.stack([column_sum] * lax.axis_size('col')), 'col', 0, 0)]
    all_gather x3 -> x0, blocking collectives: 132 us -> none  [on_device(): full_sum = lax.all_gather(column_sum, 'col', axis=1, tiled=True)]
where the time goes in v1:
time: 794 us; the launch traced here: 793 us
  blocking collectives  772 us (97%)
  matrix products  18.2 us (2%)
    psum x3, blocking collectives, on_device(): total_sum = lax.psum(pending, 'col')  289 us
    psum x3, blocking collectives, on_device(): column_sum = lax.psum(back_pending, 'row')  170 us
    all_to_all x3, blocking collectives, on_device(): lax.all_to_all(jnp.stack([column_sum] * lax.axis_size('col')), 'col', 0, 0)  160 us
    psum x1, blocking collectives, on_device(): coords = lax.psum(partial_coords, ('row', 'col'))  98.6 us
    all_gather x3, blocking collectives, on_device(): whole = lax.all_gather(fresh, 'row', axis=1, tiled=True)  54.2 us

profile of v1, /device:TPU:1, one launch (start us, length us, event | category | flops | bytes accessed | tf_op | source)
XLA Modules:
  0.0 793.1 jit_solution(6747527113295137334)
XLA Ops:
  0.6 0.0 copy-start
  0.6 0.0 copy-start.2
  0.7 0.0 copy-start.1
  0.7 0.9 select_reduce_fusion
  1.6 0.1 broadcast_bitcast_fusion
  1.7 2.0 select_convert_fusion.5
  3.7 19.7 %all_gather.9 = bf16[8,16384]{1,0:T(8,128)(2,1)S(1)} all-gather(bf16[8,1024]{1,0:T(8,128)(2,1)S(1)} %get-tuple-element.14), channel_id=1, replica_groups=mesh['row'=16,'col'=32] {'row'}, dimensions={1}, use_global_device_ids=true | all-gather | bytes 278528 | tf_op jit(solution)/shard_map/all_gather | solution.py:40
  23.3 1.6 fusion.64
  24.9 99.0 %psum.49 = f32[8,1024]{1,0:T(8,128)S(1)} all-reduce(f32[8,1024]{1,0:T(8,128)S(1)} %fusion.64), channel_id=1, replica_groups=mesh['row'=16,'col'=32] {'col'}, use_global_device_ids=true, to_apply=%region_1.2 | all-reduce | flops 8192 | bytes 65536 | tf_op jit(solution)/shard_map/psum | solution.py:29
  123.9 0.0 copy-done.2
  123.9 2.0 select_convert_fusion.4
  125.9 17.9 %all_gather.10 = bf16[8,16384]{1,0:T(8,128)(2,1)S(1)} all-gather(bf16[8,1024]{1,0:T(8,128)(2,1)S(1)} %get-tuple-element.8), channel_id=1, replica_groups=mesh['row'=16,'col'=32] {'row'}, dimensions={1}, use_global_device_ids=true | all-gather | bytes 278528 | tf_op jit(solution)/shard_map/all_gather | solution.py:40
  143.8 0.0 copy-done.1
  143.8 0.4 convolution_add_fusion.1
  144.2 95.2 %psum.50 = f32[8,1024]{1,0:T(8,128)S(1)} all-reduce(f32[8,1024]{1,0:T(8,128)S(1)} %convolution_add_fusion.1), channel_id=1, replica_groups=mesh['row'=16,'col'=32] {'col'}, use_global_device_ids=true, to_apply=%region_2.3 | all-reduce | flops 8192 | bytes 65536 | tf_op jit(solution)/shard_map/psum | solution.py:29
  239.4 2.0 select_convert_fusion.3
  241.4 16.6 %all_gather.11 = bf16[8,16384]{1,0:T(8,128)(2,1)S(1)} all-gather(bf16[8,1024]{1,0:T(8,128)(2,1)S(1)} %get-tuple-element.17), channel_id=1, replica_groups=mesh['row'=16,'col'=32] {'row'}, dimensions={1}, use_global_device_ids=true | all-gather | bytes 278528 | tf_op jit(solution)/shard_map/all_gather | solution.py:40
  258.0 0.4 convolution_add_fusion
  258.4 94.9 %psum.51 = f32[8,1024]{1,0:T(8,128)S(1)} all-reduce(f32[8,1024]{1,0:T(8,128)S(1)} %convolution_add_fusion), channel_id=1, replica_groups=mesh['row'=16,'col'=32] {'col'}, use_global_device_ids=true, to_apply=%region_3.4 | all-reduce | flops 8192 | bytes 65536 | tf_op jit(solution)/shard_map/psum | solution.py:29
  353.3 2.0 bitcast_select_fusion.5
  355.3 1.6 fusion.22
  356.9 0.2 fusion.40
  357.1 58.2 %psum.52 = f32[8,512]{1,0:T(8,128)S(1)} all-reduce(f32[8,512]{1,0:T(8,128)S(1)} %fusion.40), channel_id=1, replica_groups=mesh['row'=16,'col'=32] {'row'}, use_global_device_ids=true, to_apply=%region_4.5 | all-reduce | flops 4096 | bytes 32768 | tf_op jit(solution)/shard_map/psum | solution.py:47
  415.4 59.4 %all_to_all.15 = f32[32,8,512]{2,1,0:T(8,128)S(1)} all-to-all(f32[32,8,512]{2,1,0:T(8,128)S(1)} %stack.6), channel_id=1, replica_groups=mesh['row'=16,'col'=32] {'col'}, dimensions={0} | all-to-all | bytes 1048576 | tf_op jit(solution)/shard_map/all_to_all | solution.py:49
  474.8 1.6 bitcast_select_fusion.3
  476.4 0.2 convolution_add_fusion.3
  476.6 56.1 %psum.53 = f32[8,512]{1,0:T(8,128)S(1)} all-reduce(f32[8,512]{1,0:T(8,128)S(1)} %convolution_add_fusion.3), channel_id=1, replica_groups=mesh['row'=16,'col'=32] {'row'}, use_global_device_ids=true, to_apply=%region_5.6 | all-reduce | flops 4096 | bytes 32768 | tf_op jit(solution)/shard_map/psum | solution.py:47
  532.8 50.1 %all_to_all.16 = f32[32,8,512]{2,1,0:T(8,128)S(1)} all-to-all(f32[32,8,512]{2,1,0:T(8,128)S(1)} %stack.7), channel_id=1, replica_groups=mesh['row'=16,'col'=32] {'col'}, dimensions={0} | all-to-all | bytes 1048576 | tf_op jit(solution)/shard_map/all_to_all | solution.py:49
  582.9 0.0 copy-start.4
  582.9 0.0 copy-start.5
  582.9 1.6 fusion.18
  584.5 0.2 convolution_add_fusion.2
  584.7 55.6 %psum.54 = f32[8,512]{1,0:T(8,128)S(1)} all-reduce(f32[8,512]{1,0:T(8,128)S(1)} %convolution_add_fusion.2), channel_id=1, replica_groups=mesh['row'=16,'col'=32] {'row'}, use_global_device_ids=true, to_apply=%region_6.7 | all-reduce | flops 4096 | bytes 32768 | tf_op jit(solution)/shard_map/psum | solution.py:47
  640.4 50.9 %all_to_all.17 = f32[32,8,512]{2,1,0:T(8,128)S(1)} all-to-all(f32[32,8,512]{2,1,0:T(8,128)S(1)} %stack.8), channel_id=1, replica_groups=mesh['row'=16,'col'=32] {'col'}, dimensions={0} | all-to-all | bytes 1048576 | tf_op jit(solution)/shard_map/all_to_all | solution.py:49
  691.3 1.6 bitcast_select_fusion.1
  692.9 0.0 copy-start.3
  692.9 0.0 copy-done
  692.9 0.0 copy-done.4
  692.9 0.0 copy-done.5
  692.9 0.6 fusion.2
  693.5 98.6 %psum.55 = bf16[8,1024]{1,0:T(8,128)(2,1)S(1)} all-reduce(f32[8,1024]{1,0:T(8,128)S(1)} %fusion.2), channel_id=1, replica_groups=mesh['row'=16,'col'=32] {'row','col'}, use_global_device_ids=true, to_apply=%region_7.8 | all-reduce | flops 8192 | bytes 49152 | tf_op jit(solution)/shard_map/psum | solution.py:69
  792.1 0.4 fusion.7
  792.5 0.0 copy-done.3
  792.5 0.7 copy.11
  (5 shorter events, 0.2 us)
Async XLA Ops:
  0.6 692.2 %copy-start = (bf16[1024,1,1024]{2,0,1:T(8,128)(2,1)S(1)}, bf16[1024,1,1024]{2,0,1:T(8,128)(2,1)}, u32[]{:S(2)}) copy-start(bf16[1024,1,1024]{2,0,1:T(8,128)(2,1)} %param.13) | copy-start | bytes 6291460
  0.6 123.3 %copy-start.2 = (f32[8,1024]{1,0:T(8,128)S(1)}, f32[8,1024]{1,0:T(8,128)}, u32[]{:S(2)}) copy-start(f32[8,1024]{1,0:T(8,128)} %param.9) | copy-start | bytes 98308
  0.7 143.2 %copy-start.1 = (bf16[1024,512]{1,0:T(8,128)(2,1)S(1)}, bf16[1024,512]{1,0:T(8,128)(2,1)}, u32[]{:S(2)}) copy-start(bf16[1024,512]{1,0:T(8,128)(2,1)} %param.7) | copy-start | bytes 3145732
  582.9 110.0 %copy-start.4 = (f32[1,1024]{1,0:T(1,128)S(1)}, f32[1,1024]{1,0:T(1,128)}, u32[]{:S(2)}) copy-start(f32[1,1024]{1,0:T(1,128)} %param.11) | copy-start | bytes 12292
  582.9 110.0 %copy-start.5 = (f32[1,1024]{1,0:T(1,128)S(1)}, f32[1,1024]{1,0:T(1,128)}, u32[]{:S(2)}) copy-start(f32[1,1024]{1,0:T(1,128)} %param.12) | copy-start | bytes 12292
  692.9 99.6 %copy-start.3 = (f32[8,1024]{1,0:T(8,128)}, f32[8,1024]{1,0:T(8,128)S(1)}, u32[]{:S(2)}) copy-start(f32[8,1024]{1,0:T(8,128)S(1)} %get-tuple-element.23) | copy-start | bytes 98308
